TPU v7x, 32 devices: a whole 2x2x4 slice. The times are simulated.
32 devices in a mesh: samp: 8 (over z, core), chan: 4 (over y, x).
Axes of the slice: x: 2, y: 2, z: 4, core: 2. Of those that a mesh axis runs over, the one named last changes fastest.
Arguments:
- out_cot: bfloat16 [8, 256, 4096], P('samp', 'chan'), may hold values from -6 to 6
- mix_weight: bfloat16 [256, 256], replicated, may hold values from -0.375 to 0.375
- corr_kernels: float32 [2, 12, 256, 64], P(None, None, 'chan'), may hold values from -0.75 to 0.75
- momentum: int32 [8], P('samp'), may hold values from 0 to 11
- spin_up: int32 [8, 4096], P('samp', 'chan'), may hold values 0 or 1
- layer_input: bfloat16 [8, 256, 4096], P('samp', None, 'chan'), may hold values from -6 to 6
- pre_one: bfloat16 [8, 256, 4096], P('samp', None, 'chan'), may hold values from -6 to 6
- pre_two: bfloat16 [8, 256, 4096], P('samp', None, 'chan'), may hold values from -6 to 6
- conv_weight: bfloat16 [3, 9, 256, 256], replicated, may hold values from -0.125 to 0.125
- dilation: int32 [3, 256], replicated, may hold values from 1 to 4, as said below
Outputs:
- input_grad: bfloat16 [8, 256, 4096], P('samp', None, 'chan')
- weight_grad: float32 [3, 9, 256, 256], P(None, None, 'chan')
Inputs may be any that keep to these rules, and one draw needn't show every extreme that they name: Some channel of every convolution has dilation 4.
All inputs are finite; a program needn't handle non-finite values. No bound on the sum of `spin_up` on one device may be relied on, other than what follows from the above.
Results may differ from a plain program's by a relative error of at most 0.02.
Values may be sent and summed in bfloat16 or wider, within the bound.
A program may use at most 64 MiB of HBM per device.

v0:
```python
import math
import jax
import jax.numpy as jnp
from jax import lax
from jax.sharding import PartitionSpec as P

SIDE = 64
LAYERS = 3
MAXDIL = 4


def with_halo(shard, sides, width):
    for axis, dim in sides:
        size, length = (lax.axis_size(axis), shard.shape[dim])
        up = [(i, (i + 1) % size) for i in range(size)]
        down = [(j, i) for i, j in up]
        last = lax.slice_in_dim(shard, length - width, length, axis=dim)
        leading = lax.slice_in_dim(shard, 0, width, axis=dim)
        before = lax.ppermute(last, axis, up)
        after = lax.ppermute(leading, axis, down)
        shard = jnp.concatenate([before, shard, after], axis=dim)
    return shard


def column_shift(values, step_size, lattice_side, column):
    if step_size == 0:
        return values
    inside = (column - step_size >= 0) & (column - step_size < lattice_side)
    wrapped = step_size - lattice_side if step_size > 0 else step_size + lattice_side
    return jnp.where(inside, jnp.roll(values, step_size, axis=2), jnp.roll(values, wrapped, axis=2))


def on_device(
    out_cot,
    mix_weight,
    corr_kernels,
    momentum,
    spin_up,
    layer_input,
    pre_one,
    pre_two,
    conv_weight,
    dilation,
):
    highest = lax.Precision.HIGHEST
    sample_count = out_cot.shape[0]
    chan_block = out_cot.shape[1]
    site_count = out_cot.shape[2]
    sectors = corr_kernels.shape[1]
    lattice_side = corr_kernels.shape[3]
    slab_cells = layer_input.shape[2]
    own_start = lax.axis_index("chan") * chan_block
    own_rows = lax.dynamic_slice_in_dim(mix_weight, own_start, chan_block, 0)
    input_cot = lax.psum_scatter(
        jnp.einsum("oc,son->csn", own_rows, out_cot, preferred_element_type=jnp.float32),
        "chan",
        scatter_dimension=0,
        tiled=True,
    )
    onehot = (momentum[:, None] == jnp.arange(sectors, dtype=jnp.int32)[None, :]).astype(
        jnp.float32
    )
    picked = jnp.einsum("sk,akci->acsi", onehot, corr_kernels, precision=highest)
    positions = jnp.arange(lattice_side, dtype=jnp.int32)
    circ_table = (
        (positions[None, None, :] - positions[None, :, None]) % lattice_side
        == positions[:, None, None]
    ).astype(jnp.float32)
    circulant = jnp.einsum("acsi,ixy->acsxy", picked, circ_table, precision=highest)
    grid_values = input_cot.reshape(chan_block, sample_count, lattice_side, lattice_side)
    halfway = jnp.einsum("csxX,csxy->csXy", circulant[0], grid_values, precision=highest)
    corr_grad = jnp.einsum("csXy,csyY->scXY", halfway, circulant[1], precision=highest)
    corr_grad = corr_grad.reshape(sample_count, chan_block, site_count).astype(jnp.bfloat16)
    regrouped = lax.all_to_all(corr_grad, "chan", split_axis=2, concat_axis=1, tiled=True)
    spin_gate = jnp.where(spin_up == 1, 1.5, 0.5).astype(jnp.float32)[:, None, :]
    grad_now = (regrouped.astype(jnp.float32) * spin_gate).astype(jnp.bfloat16)
    halo_cells = MAXDIL * SIDE
    column = jnp.arange(slab_cells, dtype=jnp.int32) % lattice_side
    norm_factor = 1.0 / math.sqrt(sample_count * lax.axis_size("samp") * site_count)
    layer_grads = [None] * LAYERS
    input_grad = None
    for conv_level in range(LAYERS - 1, -1, -1):
        slope_base = None
        if conv_level == 0:
            layer_values = layer_input
        else:
            saved_pre = pre_one if conv_level == 1 else pre_two
            slope_base = jnp.tanh(saved_pre.astype(jnp.float32))
            layer_values = slope_base.astype(jnp.bfloat16)
        padded = with_halo(grad_now, (("chan", 2),), halo_cells)
        back_sum = jnp.zeros(grad_now.shape, jnp.float32)
        tap_grads = []
        for row_step in (-1, 0, 1):
            for col_step in (-1, 0, 1):
                tap_index = (row_step + 1) * 3 + col_step + 1
                if row_step == 0 and col_step == 0:
                    combined = grad_now
                else:
                    combined = None
                    for dilate in range(1, MAXDIL + 1):
                        slice_begin = halo_cells - row_step * dilate * lattice_side
                        shifted = column_shift(
                            padded[:, :, slice_begin : slice_begin + slab_cells],
                            col_step * dilate,
                            lattice_side,
                            column,
                        )
                        if combined is None:
                            combined = shifted
                        else:
                            chosen_mask = (dilation[conv_level] == dilate)[None, :, None]
                            combined = jnp.where(chosen_mask, shifted, combined)
                back_sum = back_sum + jnp.einsum(
                    "oc,son->scn",
                    conv_weight[conv_level, tap_index],
                    combined,
                    preferred_element_type=jnp.float32,
                )
                tap_grads.append(
                    jnp.einsum(
                        "son,scn->oc", combined, layer_values, preferred_element_type=jnp.float32
                    )
                    * norm_factor
                )
        local_grad = jnp.stack(tap_grads)
        reduced = lax.psum_scatter(
            local_grad.astype(jnp.bfloat16), "chan", scatter_dimension=1, tiled=True
        )
        layer_grads[conv_level] = lax.psum(reduced, "samp").astype(jnp.float32)
        if conv_level > 0:
            grad_now = (back_sum * (1.0 - slope_base * slope_base)).astype(jnp.bfloat16)
        else:
            input_grad = back_sum.astype(jnp.bfloat16)
    weight_grad = jnp.stack(layer_grads)
    return (input_grad, weight_grad)


def solution(mesh):
    in_specs = (
        P("samp", "chan", None),
        P(),
        P(None, None, "chan", None),
        P("samp"),
        P("samp", "chan"),
        P("samp", None, "chan"),
        P("samp", None, "chan"),
        P("samp", None, "chan"),
        P(),
        P(),
    )
    out_specs = (P("samp", None, "chan"), P(None, None, "chan", None))
    return jax.shard_map(
        on_device, mesh=mesh, in_specs=in_specs, out_specs=out_specs, check_vma=False
    )
```

profile of v0, /device:TPU:0, one launch (start us, length us, event | category | flops | bytes accessed | tf_op | source)
XLA Modules:
  0.0 344.3 jit_solution(6769106226334867354)
XLA Ops:
  7.2 3.8 %convolution_bitcast_fusion = f32[256,1,4096]{2,0,1:T(8,128)} fusion(bf16[1,64,4096]{2,1,0:T(8,128)(2,1)} %param.10, bf16[256,256]{1,0:T(8,128)(2,1)} %param.11, s32[]{:T(128)S(6)} %select_n.3285), kind=kOutput, calls=%fused_computation | convolution fusion | flops 134217728 | bytes 4751364 | tf_op jit(solution)/shard_map/oc,son->csn/dot_general | solution.py:55
  12.7 1.8 fusion.5
  14.5 2.3 slice_bitcast_fusion
  16.8 49.8 %reduce-scatter.5.cloned.1.call-done = f32[64,1,4096]{2,0,1:T(8,128)} async-done(((f32[256,1,4096]{2,0,1:T(8,128)}), f32[64,1,4096]{2,0,1:T(8,128)}) %reduce-scatter.5.cloned.1.call-update) | async-done | bytes 1048592 | tf_op jit(solution)/shard_map/reduce_scatter | solution.py:54
  66.7 2.2 reshape.16731
  68.8 6.2 %fusion.2 = f32[64,64,64]{2,1,0:T(8,128)S(1)} fusion(f32[64,64,64]{2,1,0:T(8,128)S(1)} %reshape.16731, f32[64,64,64]{2,0,1:T(8,128)} %get-tuple-element.25), kind=kOutput, calls=%fused_computation.119 | convolution fusion | flops 201326592 | bytes 3145728 | tf_op jit(solution)/shard_map/csxX,csxy->csXy/dot_general | solution.py:71
  75.0 3.3 fusion.7
  79.2 2.8 copy.42
  82.5 23.6 %reduce.18 = bf16[4096,64]{1,0:T(8,128)(2,1)} reduce(bf16[4096,1,64]{2,1,0:T(2,128)(2,1)S(1)} %bitcast.976, bf16[]{:T(256)} %broadcast.4323), dimensions={1}, to_apply=%bitcast.918.reduce_sub_computation | reduce | bytes 1048578
  106.1 2.7 reshape.16776
  108.7 3.5 %all-to-all-start = ((bf16[4,2,32768]{2,1,0:T(2,128)(2,1)}), bf16[4,2,32768]{2,1,0:T(2,128)(2,1)S(1)}, u32[]{:S(2)}, u32[]{:S(2)}) async-start(bf16[4,2,32768]{2,1,0:T(2,128)(2,1)} %reshape.16776), calls=%async_computation.1 | async-start | bytes 1048576 | tf_op jit(solution)/shard_map/all_to_all | solution.py:74
  114.4 6.1 %all-to-all-done = bf16[4,2,32768]{2,1,0:T(2,128)(2,1)S(1)} async-done(((bf16[4,2,32768]{2,1,0:T(2,128)(2,1)}), bf16[4,2,32768]{2,1,0:T(2,128)(2,1)S(1)}, u32[]{:S(2)}, u32[]{:S(2)}) %all-to-all-start) | async-done | bytes 524320 | tf_op jit(solution)/shard_map/all_to_all | solution.py:74
  121.3 2.3 copy.43
  126.2 1.5 collective-permute-start.1
  127.7 1.9 collective-permute-start
  129.6 4.8 %collective-permute-done = bf16[1,256,256]{1,2,0:T(8,128)(2,1)S(1)} collective-permute-done((bf16[1,256,256]{1,2,0:T(8,128)(2,1)S(1)}, bf16[1,256,256]{1,2,0:T(8,128)(2,1)S(1)}, u32[]{:S(2)}, u32[]{:S(2)}) %collective-permute-start) | collective-permute-done | bytes 131104 | tf_op jit(solution)/shard_map/ppermute | solution.py:20
  137.4 3.0 fusion.252
  143.4 3.0 fusion.256
  147.6 3.0 fusion.260
  151.8 1.3 convolution_add_fusion.20
  153.1 3.0 fusion.264
  157.4 3.0 fusion.268
  162.9 3.0 fusion.272
  165.9 1.2 fusion.14
  168.8 2.0 collective-permute-start.2
  177.7 3.0 fusion.276
  183.7 3.0 fusion.280
  186.7 1.2 convolution_add_fusion.14
  187.9 3.0 fusion.284
  193.4 3.0 fusion.288
  197.6 3.0 fusion.292
  203.1 3.0 fusion.296
  206.2 1.2 fusion.15
  208.5 2.0 collective-permute-start.4
  218.1 3.0 fusion.300
  223.8 3.0 fusion.304
  227.8 3.0 fusion.308
  232.9 3.0 fusion.312
  236.8 3.0 fusion.316
  241.9 3.0 fusion.320
  249.6 1.3 convolution_add_fusion.5
  250.8 1.3 convolution_add_fusion.4
  252.1 1.2 convolution_add_fusion.3
  253.4 1.3 convolution_add_fusion.2
  254.7 20.1 %reduce-scatter.7.cloned.1.call-done = bf16[9,64,256]{2,1,0:T(8,128)(2,1)} async-done(((bf16[9,256,256]{2,1,0:T(8,128)(2,1)}), bf16[9,64,256]{2,1,0:T(8,128)(2,1)}) %reduce-scatter.7.cloned.1.call-update) | async-done | bytes 294928 | tf_op jit(solution)/shard_map/reduce_scatter | solution.py:126
  276.1 1.3 fusion.17
  278.4 56.7 %all-reduce.3.cloned.1.call-done = (bf16[1,9,64,256]{3,2,1,0:T(8,128)(2,1)}, bf16[1,9,64,256]{3,2,1,0:T(8,128)(2,1)}, bf16[1,9,64,256]{3,2,1,0:T(8,128)(2,1)}) async-done(((bf16[1,9,64,256]{3,2,1,0:T(8,128)(2,1)}, bf16[1,9,64,256]{3,2,1,0:T(8,128)(2,1)}, bf16[1,9,64,256]{3,2,1,0:T(8,128)(2,1)}), (bf16[1,9,64,256]{3,2,1,0:T(8,128)(2,1)}, bf16[1,9,64,256]{3,2,1,0:T(8,128)(2,1)}, ...) | async-done | bytes 884752 | tf_op jit(solution)/shard_map/psum | solution.py:129
  335.0 2.5 maximum_convert_fusion
  (226 shorter events, 61.1 us)
Async XLA Ops:
  7.2 4.7 %copy-start = (f32[2,12,64,64]{3,2,1,0:T(8,128)S(1)}, f32[2,12,64,64]{3,2,1,0:T(8,128)}, u32[]{:S(2)}) copy-start(f32[2,12,64,64]{3,2,1,0:T(8,128)} %param.12) | copy-start | bytes 1179652
  7.2 59.5 %reduce-scatter.5.cloned.1.call-start = ((), (), s32[]{:S(2)}) async-start(), calls=%async_computation.5 | async-start | bytes 5242880 | tf_op jit(solution)/shard_map/reduce_scatter | solution.py:54
  68.8 6.2 %copy-start.2 = (f32[64,64,64]{2,0,1:T(8,128)S(1)}, f32[64,64,64]{2,0,1:T(8,128)}, u32[]{:S(2)}) copy-start(f32[64,64,64]{2,0,1:T(8,128)} %get-tuple-element.24) | copy-start | bytes 3145732
  106.1 6.2 %copy-start.15 = (bf16[1,256,1024]{2,1,0:T(8,128)(2,1)S(1)}, bf16[1,256,1024]{2,1,0:T(8,128)(2,1)}, u32[]{:S(2)}) copy-start(bf16[1,256,1024]{2,1,0:T(8,128)(2,1)} %param.16) | copy-start | bytes 1572868
  106.1 7.2 %copy-start.16 = (bf16[1,256,1024]{2,1,0:T(8,128)(2,1)S(1)}, bf16[1,256,1024]{2,1,0:T(8,128)(2,1)}, u32[]{:S(2)}) copy-start(bf16[1,256,1024]{2,1,0:T(8,128)(2,1)} %param.17) | copy-start | bytes 1572868
  106.1 8.2 %copy-start.18 = (s32[3,256]{1,0:T(4,128)S(1)}, s32[3,256]{1,0:T(4,128)}, u32[]{:S(2)}) copy-start(s32[3,256]{1,0:T(4,128)} %param.19) | copy-start | bytes 9220
  106.1 8.3 %copy-start.17 = (s32[1,1024]{1,0:T(1,128)S(1)}, s32[1,1024]{1,0:T(1,128)}, u32[]{:S(2)}) copy-start(s32[1,1024]{1,0:T(1,128)} %param.14) | copy-start | bytes 12292
  108.7 11.7 %all-to-all-start = ((bf16[4,2,32768]{2,1,0:T(2,128)(2,1)}), bf16[4,2,32768]{2,1,0:T(2,128)(2,1)S(1)}, u32[]{:S(2)}, u32[]{:S(2)}) async-start(bf16[4,2,32768]{2,1,0:T(2,128)(2,1)} %reshape.16776), calls=%async_computation.1 | async-start | bytes 1048576 | tf_op jit(solution)/shard_map/all_to_all | solution.py:74
  112.2 142.5 %reduce-scatter.11.cloned.1.call-start = ((), (), s32[]{:S(2)}) async-start(), calls=%async_computation.8 | async-start | bytes 1474560 | tf_op jit(solution)/shard_map/reduce_scatter | solution.py:126
  126.2 8.3 %collective-permute-start.1 = (bf16[1,256,256]{1,2,0:T(8,128)(2,1)S(1)}, bf16[1,256,256]{1,2,0:T(8,128)(2,1)S(1)}, u32[]{:S(2)}, u32[]{:S(2)}) collective-permute-start(bf16[1,256,256]{1,2,0:T(8,128)(2,1)S(1)} %get-tuple-element.324), channel_id=1, source_target_pairs={{0,1},{1,2},{2,3},{3,0},{4,5},{5,6},{6,7},{7,4},{8,9},{9,10},{10,1... | collective-permute-start | bytes 393224 | tf_op jit(solution)/shard_map/ppermute | solution.py:19
  127.7 6.7 %collective-permute-start = (bf16[1,256,256]{1,2,0:T(8,128)(2,1)S(1)}, bf16[1,256,256]{1,2,0:T(8,128)(2,1)S(1)}, u32[]{:S(2)}, u32[]{:S(2)}) collective-permute-start(bf16[1,256,256]{1,2,0:T(8,128)(2,1)S(1)} %get-tuple-element.325), channel_id=1, source_target_pairs={{1,0},{2,1},{3,2},{0,3},{5,4},{6,5},{7,6},{4,7},{9,8},{10,9},{11,1... | collective-permute-start | bytes 393224 | tf_op jit(solution)/shard_map/ppermute | solution.py:20
  162.9 3.0 copy-start.8
  167.7 7.3 %collective-permute-start.3 = (bf16[1,256,256]{1,2,0:T(8,128)(2,1)S(1)}, bf16[1,256,256]{1,2,0:T(8,128)(2,1)S(1)}, u32[]{:S(2)}, u32[]{:S(2)}) collective-permute-start(bf16[1,256,256]{1,2,0:T(8,128)(2,1)S(1)} %get-tuple-element.258), channel_id=1, source_target_pairs={{0,1},{1,2},{2,3},{3,0},{4,5},{5,6},{6,7},{7,4},{8,9},{9,10},{10,1... | collective-permute-start | bytes 393224 | tf_op jit(solution)/shard_map/ppermute | solution.py:19
  168.8 6.1 %collective-permute-start.2 = (bf16[1,256,256]{1,2,0:T(8,128)(2,1)S(1)}, bf16[1,256,256]{1,2,0:T(8,128)(2,1)S(1)}, u32[]{:S(2)}, u32[]{:S(2)}) collective-permute-start(bf16[1,256,256]{1,2,0:T(8,128)(2,1)S(1)} %get-tuple-element.259), channel_id=1, source_target_pairs={{1,0},{2,1},{3,2},{0,3},{5,4},{6,5},{7,6},{4,7},{9,8},{10,9},{11,1... | collective-permute-start | bytes 393224 | tf_op jit(solution)/shard_map/ppermute | solution.py:20
  173.8 1.0 copy-start.13
  174.8 79.9 %reduce-scatter.9.cloned.1.call-start = ((), (), s32[]{:S(2)}) async-start(), calls=%async_computation.7 | async-start | bytes 1474560 | tf_op jit(solution)/shard_map/reduce_scatter | solution.py:126
  203.1 3.0 copy-start.7
  207.6 7.8 %collective-permute-start.5 = (bf16[1,256,256]{1,2,0:T(8,128)(2,1)S(1)}, bf16[1,256,256]{1,2,0:T(8,128)(2,1)S(1)}, u32[]{:S(2)}, u32[]{:S(2)}) collective-permute-start(bf16[1,256,256]{1,2,0:T(8,128)(2,1)S(1)} %get-tuple-element.192), channel_id=1, source_target_pairs={{0,1},{1,2},{2,3},{3,0},{4,5},{5,6},{6,7},{7,4},{8,9},{9,10},{10,1... | collective-permute-start | bytes 393224 | tf_op jit(solution)/shard_map/ppermute | solution.py:19
  208.5 6.8 %collective-permute-start.4 = (bf16[1,256,256]{1,2,0:T(8,128)(2,1)S(1)}, bf16[1,256,256]{1,2,0:T(8,128)(2,1)S(1)}, u32[]{:S(2)}, u32[]{:S(2)}) collective-permute-start(bf16[1,256,256]{1,2,0:T(8,128)(2,1)S(1)} %get-tuple-element.193), channel_id=1, source_target_pairs={{1,0},{2,1},{3,2},{0,3},{5,4},{6,5},{7,6},{4,7},{9,8},{10,9},{11,1... | collective-permute-start | bytes 393224 | tf_op jit(solution)/shard_map/ppermute | solution.py:20
  213.9 1.0 copy-start.14
  215.0 59.8 %reduce-scatter.7.cloned.1.call-start = ((), (), s32[]{:S(2)}) async-start(), calls=%async_computation.6 | async-start | bytes 1474560 | tf_op jit(solution)/shard_map/reduce_scatter | solution.py:126
  218.1 3.0 copy-start.19
  222.7 4.1 %copy-start.11 = (bf16[256,1024]{0,1:T(8,128)(2,1)}, bf16[256,1024]{0,1:T(8,128)(2,1)S(1)}, u32[]{:S(2)}) copy-start(bf16[256,1024]{0,1:T(8,128)(2,1)S(1)} %get-tuple-element.123) | copy-start | bytes 1572868
  222.7 18.2 %copy-start.9 = (bf16[256,1024]{0,1:T(8,128)(2,1)}, bf16[256,1024]{0,1:T(8,128)(2,1)S(1)}, u32[]{:S(2)}) copy-start(bf16[256,1024]{0,1:T(8,128)(2,1)S(1)} %get-tuple-element.122) | copy-start | bytes 1572868
  235.8 4.0 %copy-start.3 = (bf16[256,1024]{0,1:T(8,128)(2,1)}, bf16[256,1024]{0,1:T(8,128)(2,1)S(1)}, u32[]{:S(2)}) copy-start(bf16[256,1024]{0,1:T(8,128)(2,1)S(1)} %fusion.312) | copy-start | bytes 1572868
  239.8 2.0 copy-start.5
  244.8 2.3 copy-start.12
  245.9 89.1 %all-reduce.3.cloned.1.call-start = ((), (), s32[]{:S(2)}) async-start(), calls=%async_computation.9 | async-start | bytes 1769472 | tf_op jit(solution)/shard_map/psum | solution.py:129
  249.6 2.6 copy-start.4
  250.8 2.5 copy-start.6
  253.4 21.5 %copy-start.10 = (bf16[256,1024]{0,1:T(8,128)(2,1)S(1)}, bf16[256,1024]{0,1:T(8,128)(2,1)}, u32[]{:S(2)}) copy-start(bf16[256,1024]{0,1:T(8,128)(2,1)} %copy-done.9) | copy-start | bytes 1572868
  276.1 61.5 %copy-start.1 = (f32[2,12,64,64]{3,2,1,0:T(8,128)S(1)}, f32[2,12,64,64]{3,2,1,0:T(8,128)}, u32[]{:S(2)}) copy-start(f32[2,12,64,64]{3,2,1,0:T(8,128)} %param.12) | copy-start | bytes 1179652
Sparse Core Ops, SparseCore 0:
  11.2 55.3 reduce-scatter.4
  174.9 27.8 reduce-scatter.10
  215.1 28.0 reduce-scatter.8
  246.3 28.5 reduce-scatter.6
  277.4 57.5 all-reduce.2
where the time goes:
time: 348 us; the launch traced here: 344 us
  waiting for transfers between devices  138 us (40%)
  other arithmetic  90.3 us (26%)
  matrix products  64.6 us (19%)
  local copies, waits for them, and re-layouts  22.2 us (6%)
  between operations  16.2 us (5%)
  starting transfers between devices  13.4 us (4%)
    psum x1, waiting for transfers between devices, on_device(): layer_grads[conv_level] = lax.psum(reduced, 'samp').astype(jnp.float32)  56.7 us
    select_n x18, other arithmetic, on_device(): combined = jnp.where(chosen_mask, shifted, combined)  54 us
    reduce_scatter x1, waiting for transfers between devices, on_device(): lax.psum_scatter(jnp.einsum('oc,son->csn', own_rows, out_cot, preferred_e...  49.8 us
    dot_general x27, matrix products, on_device(): jnp.einsum('oc,son->scn', conv_weight[conv_level, tap_index], combined, p...  32.9 us
    unnamed x1, other arithmetic  23.6 us
    reduce_scatter x3, waiting for transfers between devices, on_device(): lax.psum_scatter(local_grad.astype(jnp.bfloat16), 'chan', scatter_dimensi...  20.1 us
    dot_general x27, matrix products, on_device(): jnp.einsum('son,scn->oc', combined, layer_values, preferred_element_type=...  15.7 us
    unnamed x46, local copies, waits for them, and re-layouts  9.22 us
  transfers between devices with their start and end apart: 12, of which 5 were waited for; matrix products, arithmetic and copies ran while one was open for 26% of the time, Pallas kernels for 0%

commit v1 on v0

--- a/solution.py
+++ b/solution.py
@@ -7,6 +7,19 @@
 SIDE = 64
 LAYERS = 3
 MAXDIL = 4
+
+
+def _edit_samples_all(unit, axis_no, z):
+    current_block, y2 = (unit.shape[:axis_no], unit.shape[axis_no + 1 :])
+    inter = jnp.moveaxis(unit.reshape(*current_block, z, -1, *y2), axis_no, 0)
+    return inter
+
+
+def follow_cycles(xs, ndim_at):
+    known = list(xs.shape[1:])
+    known[ndim_at] *= xs.shape[0]
+    right_arr = jnp.moveaxis(xs, 0, ndim_at).reshape(known)
+    return right_arr
 
 
 def with_halo(shard, sides, width):
@@ -71,7 +84,25 @@
     halfway = jnp.einsum("csxX,csxy->csXy", circulant[0], grid_values, precision=highest)
     corr_grad = jnp.einsum("csXy,csyY->scXY", halfway, circulant[1], precision=highest)
     corr_grad = corr_grad.reshape(sample_count, chan_block, site_count).astype(jnp.bfloat16)
-    regrouped = lax.all_to_all(corr_grad, "chan", split_axis=2, concat_axis=1, tiled=True)
+
+    def expand_layers_all(my_data, mesh_ax, t0, x_in):
+        field_out, r2 = (lax.axis_size(mesh_ax), lax.axis_index(mesh_ax))
+        prior = _edit_samples_all(my_data, t0, field_out)
+        fields = [prior[r2]]
+        for kk in range(1, field_out):
+            out_arr = prior[r2 ^ kk]
+            fields.append(
+                lax.ppermute(
+                    out_arr,
+                    axis_name=mesh_ax,
+                    perm=[(tick, tick ^ kk) for tick in range(field_out)],
+                )
+            )
+        prior = jnp.stack(fields)[r2 ^ jnp.arange(field_out)]
+        x_next = follow_cycles(prior, x_in)
+        return x_next
+
+    regrouped = expand_layers_all(corr_grad, "chan", 2, 1)
     spin_gate = jnp.where(spin_up == 1, 1.5, 0.5).astype(jnp.float32)[:, None, :]
     grad_now = (regrouped.astype(jnp.float32) * spin_gate).astype(jnp.bfloat16)
     halo_cells = MAXDIL * SIDE

time: 348 us -> 321 us (0.922)
  other arithmetic: 90.3 us -> 67.3 us
  local copies, waits for them, and re-layouts: 22.2 us -> 13.4 us
  matrix products: 64.6 us -> 70.4 us
    unnamed x1 -> x0, other arithmetic: 23.6 us -> none
    all_to_all x1 -> x0, waiting for transfers between devices: 6.09 us -> none  [on_device(): lax.all_to_all(corr_grad, 'chan', split_axis=2, concat_axis=1, tiled=True)]
    unnamed x46 -> x87, local copies, waits for them, and re-layouts: 9.22 us -> 3.17 us
    dot_general x27, matrix products: 15.7 us -> 21.5 us  [on_device(): jnp.einsum('son,scn->oc', combined, layer_values, preferred_element_type=...]
    ppermute x0 -> x3, waiting for transfers between devices: none -> 4.32 us  [expand_layers_all(): lax.ppermute(out_arr, axis_name=mesh_ax, perm=[(tick, tick ^ kk) for tick...]
    ppermute x0 -> x3, starting transfers between devices: none -> 3.55 us  [expand_layers_all(): lax.ppermute(out_arr, axis_name=mesh_ax, perm=[(tick, tick ^ kk) for tick...]
  transfers between devices with their start and end apart: 12 -> 14, of which waited for: 5 -> 7; matrix products, arithmetic and copies ran while one was open for 26% -> 30% of each run, Pallas kernels for 0% -> 0%
where the time goes in v1:
time: 321 us; the launch traced here: 317 us
  waiting for transfers between devices  136 us (42%)
  matrix products  70.4 us (22%)
  other arithmetic  67.3 us (21%)
  between operations  16.4 us (5%)
  local copies, waits for them, and re-layouts  13.4 us (4%)
  starting transfers between devices  13.3 us (4%)
    psum x1, waiting for transfers between devices, on_device(): layer_grads[conv_level] = lax.psum(reduced, 'samp').astype(jnp.float32)  56.6 us
    select_n x18, other arithmetic, on_device(): combined = jnp.where(chosen_mask, shifted, combined)  54.1 us
    reduce_scatter x1, waiting for transfers between devices, on_device(): lax.psum_scatter(jnp.einsum('oc,son->csn', own_rows, out_cot, preferred_e...  49.6 us
    dot_general x27, matrix products, on_device(): jnp.einsum('oc,son->scn', conv_weight[conv_level, tap_index], combined, p...  32.8 us
    dot_general x27, matrix products, on_device(): jnp.einsum('son,scn->oc', combined, layer_values, preferred_element_type=...  21.5 us
    reduce_scatter x3, waiting for transfers between devices, on_device(): lax.psum_scatter(local_grad.astype(jnp.bfloat16), 'chan', scatter_dimensi...  19.8 us
    ppermute x3, starting transfers between devices, with_halo(): after = lax.ppermute(leading, axis, down)  7.48 us
  transfers between devices with their start and end apart: 14, of which 7 were waited for; matrix products, arithmetic and copies ran while one was open for 30% of the time, Pallas kernels for 0%

profile of v1, /device:TPU:0, one launch (start us, length us, event | category | flops | bytes accessed | tf_op | source)
XLA Modules:
  0.0 316.8 jit_solution(588304964411034784)
XLA Ops:
  7.2 3.9 %convolution_bitcast_fusion = f32[256,1,4096]{2,0,1:T(8,128)} fusion(bf16[1,64,4096]{2,1,0:T(8,128)(2,1)} %param.10, bf16[256,256]{1,0:T(8,128)(2,1)} %param.11, s32[]{:T(128)S(6)} %select_n.3307), kind=kOutput, calls=%fused_computation.1 | convolution fusion | flops 134217728 | bytes 4751364 | tf_op jit(solution)/shard_map/oc,son->csn/dot_general | solution.py:68
  12.9 1.8 fusion.5
  14.7 2.3 slice_bitcast_fusion
  17.0 49.6 %reduce-scatter.5.cloned.1.call-done = f32[64,1,4096]{2,0,1:T(8,128)} async-done(((f32[256,1,4096]{2,0,1:T(8,128)}), f32[64,1,4096]{2,0,1:T(8,128)}) %reduce-scatter.5.cloned.1.call-update) | async-done | bytes 1048592 | tf_op jit(solution)/shard_map/reduce_scatter | solution.py:67
  66.7 2.2 reshape.16786
  68.9 6.2 %fusion = f32[64,64,64]{2,1,0:T(8,128)S(1)} fusion(f32[64,64,64]{2,1,0:T(8,128)S(1)} %reshape.16786, f32[64,64,64]{2,0,1:T(8,128)} %get-tuple-element.19), kind=kOutput, calls=%fused_computation.118 | convolution fusion | flops 201326592 | bytes 3145728 | tf_op jit(solution)/shard_map/csxX,csxy->csXy/dot_general | solution.py:84
  75.0 3.3 %fusion.7 = bf16[64,64,64]{2,1,0:T(8,128)(2,1)S(1)} fusion(f32[64,64,64]{2,1,0:T(8,128)S(1)} %fusion, f32[64,64,64]{2,0,1:T(8,128)S(1)} %copy-done.2), kind=kOutput, calls=%fused_computation.125 | convolution fusion | flops 201588736 | bytes 2621440 | tf_op jit(solution)/shard_map/csXy,csyY->scXY/dot_general | solution.py:85
  80.3 1.5 collective-permute-start.2
  81.8 1.4 collective-permute-start
  85.0 2.7 collective-permute-done.2
  87.6 1.6 collective-permute-done
  90.7 1.4 collective-permute-start.4
  92.1 1.9 collective-permute-start.3
  94.0 5.5 %collective-permute-done.3 = bf16[1,256,256]{1,2,0:T(8,128)(2,1)S(1)} collective-permute-done((bf16[1,256,256]{1,2,0:T(8,128)(2,1)S(1)}, bf16[1,256,256]{1,2,0:T(8,128)(2,1)S(1)}, u32[]{:S(2)}, u32[]{:S(2)}) %collective-permute-start.3) | collective-permute-done | bytes 131104 | tf_op jit(solution)/shard_map/ppermute | solution.py:33
  102.5 3.0 fusion.252
  108.5 3.0 fusion.256
  112.8 3.0 fusion.260
  117.0 1.3 convolution_add_fusion.20
  118.2 3.0 fusion.264
  122.5 3.0 fusion.268
  125.5 1.2 convolution_add_fusion.18
  126.7 1.2 convolution_add_fusion.17
  128.0 3.0 fusion.272
  131.0 1.2 fusion.14
  133.9 2.6 collective-permute-start.5
  147.7 3.0 fusion.276
  153.6 3.0 fusion.280
  156.6 1.2 convolution_add_fusion.14
  157.8 3.0 fusion.284
  163.3 3.0 fusion.288
  167.6 3.0 fusion.292
  173.1 3.0 fusion.296
  176.1 1.2 fusion.15
  180.0 2.9 collective-permute-start.7
  190.9 3.0 fusion.300
  196.5 3.0 fusion.304
  200.6 3.0 fusion.308
  205.7 3.0 fusion.312
  209.7 3.0 fusion.316
  214.7 3.0 fusion.320
  222.5 1.3 convolution_add_fusion.5
  223.7 1.3 convolution_add_fusion.4
  225.0 1.2 convolution_add_fusion.3
  226.3 1.3 convolution_add_fusion.2
  227.6 19.8 %reduce-scatter.7.cloned.1.call-done = bf16[9,64,256]{2,1,0:T(8,128)(2,1)} async-done(((bf16[9,256,256]{2,1,0:T(8,128)(2,1)}), bf16[9,64,256]{2,1,0:T(8,128)(2,1)}) %reduce-scatter.7.cloned.1.call-update) | async-done | bytes 294928 | tf_op jit(solution)/shard_map/reduce_scatter | solution.py:157
  248.6 1.3 fusion.17
  250.9 56.6 %all-reduce.3.cloned.1.call-done = (bf16[1,9,64,256]{3,2,1,0:T(8,128)(2,1)}, bf16[1,9,64,256]{3,2,1,0:T(8,128)(2,1)}, bf16[1,9,64,256]{3,2,1,0:T(8,128)(2,1)}) async-done(((bf16[1,9,64,256]{3,2,1,0:T(8,128)(2,1)}, bf16[1,9,64,256]{3,2,1,0:T(8,128)(2,1)}, bf16[1,9,64,256]{3,2,1,0:T(8,128)(2,1)}), (bf16[1,9,64,256]{3,2,1,0:T(8,128)(2,1)}, bf16[1,9,64,256]{3,2,1,0:T(8,128)(2,1)}, ...) | async-done | bytes 884752 | tf_op jit(solution)/shard_map/psum | solution.py:160
  307.5 2.5 maximum_convert_fusion
  (270 shorter events, 63.0 us)
Async XLA Ops:
  7.2 4.8 %copy-start = (f32[2,12,64,64]{3,2,1,0:T(8,128)S(1)}, f32[2,12,64,64]{3,2,1,0:T(8,128)}, u32[]{:S(2)}) copy-start(f32[2,12,64,64]{3,2,1,0:T(8,128)} %param.12) | copy-start | bytes 1179652
  7.2 59.5 %reduce-scatter.5.cloned.1.call-start = ((), (), s32[]{:S(2)}) async-start(), calls=%async_computation.4 | async-start | bytes 5242880 | tf_op jit(solution)/shard_map/reduce_scatter | solution.py:67
  11.1 0.9 copy-start.37
  11.1 216.4 %reduce-scatter.11.cloned.1.call-start = ((), (), s32[]{:S(2)}) async-start(), calls=%async_computation.7 | async-start | bytes 1474560 | tf_op jit(solution)/shard_map/reduce_scatter | solution.py:157
  11.9 155.7 %copy-start.14 = (pred[1024]{0:T(1024)(128)(4,1)}, pred[1024]{0:T(1024)(128)(4,1)S(1)}, u32[]{:S(2)}) copy-start(pred[1024]{0:T(1024)(128)(4,1)S(1)} %get-tuple-element.324) | copy-start | bytes 3076
  11.9 155.7 %copy-start.16 = (pred[1024]{0:T(1024)(128)(4,1)}, pred[1024]{0:T(1024)(128)(4,1)S(1)}, u32[]{:S(2)}) copy-start(pred[1024]{0:T(1024)(128)(4,1)S(1)} %get-tuple-element.325) | copy-start | bytes 3076
  68.8 6.2 %copy-start.2 = (f32[64,64,64]{2,0,1:T(8,128)S(1)}, f32[64,64,64]{2,0,1:T(8,128)}, u32[]{:S(2)}) copy-start(f32[64,64,64]{2,0,1:T(8,128)} %get-tuple-element.18) | copy-start | bytes 3145732
  78.4 5.5 %copy-start.12 = (bf16[1,256,1024]{2,1,0:T(8,128)(2,1)S(1)}, bf16[1,256,1024]{2,1,0:T(8,128)(2,1)}, u32[]{:S(2)}) copy-start(bf16[1,256,1024]{2,1,0:T(8,128)(2,1)} %param.16) | copy-start | bytes 1572868
  79.0 5.1 %copy-start.13 = (bf16[1,256,1024]{2,1,0:T(8,128)(2,1)S(1)}, bf16[1,256,1024]{2,1,0:T(8,128)(2,1)}, u32[]{:S(2)}) copy-start(bf16[1,256,1024]{2,1,0:T(8,128)(2,1)} %param.17) | copy-start | bytes 1572868
  80.1 4.2 %copy-start.38 = (s32[3,256]{1,0:T(4,128)S(1)}, s32[3,256]{1,0:T(4,128)}, u32[]{:S(2)}) copy-start(s32[3,256]{1,0:T(4,128)} %param.19) | copy-start | bytes 9220
  80.3 7.4 %collective-permute-start.2 = (bf16[1,64,1024]{2,1,0:T(8,128)(2,1)S(1)}, bf16[1,64,1024]{2,1,0:T(8,128)(2,1)S(1)}, u32[]{:S(2)}, u32[]{:S(2)}) collective-permute-start(bf16[1,64,1024]{2,1,0:T(8,128)(2,1)S(1)} %bitcast.1005), channel_id=1, source_target_pairs={{0,3},{1,2},{2,1},{3,0},{4,7},{5,6},{6,5},{7,4},{8,11},{9,10},{10,... | collective-permute-start | bytes 393224 | tf_op jit(solution)/shard_map/ppermute | solution.py:95
  81.8 7.4 %collective-permute-start = (bf16[1,64,1024]{2,1,0:T(8,128)(2,1)S(1)}, bf16[1,64,1024]{2,1,0:T(8,128)(2,1)S(1)}, u32[]{:S(2)}, u32[]{:S(2)}) collective-permute-start(bf16[1,64,1024]{2,1,0:T(8,128)(2,1)S(1)} %bitcast.1004), channel_id=1, source_target_pairs={{0,1},{1,0},{2,3},{3,2},{4,5},{5,4},{6,7},{7,6},{8,9},{9,8},{10,11... | collective-permute-start | bytes 393224 | tf_op jit(solution)/shard_map/ppermute | solution.py:95
  83.2 6.1 %collective-permute-start.1 = (bf16[1,64,1024]{2,1,0:T(8,128)(2,1)S(1)}, bf16[1,64,1024]{2,1,0:T(8,128)(2,1)S(1)}, u32[]{:S(2)}, u32[]{:S(2)}) collective-permute-start(bf16[1,64,1024]{2,1,0:T(8,128)(2,1)S(1)} %bitcast.1003), channel_id=1, source_target_pairs={{0,2},{1,3},{2,0},{3,1},{4,6},{5,7},{6,4},{7,5},{8,10},{9,11},{10,... | collective-permute-start | bytes 393224 | tf_op jit(solution)/shard_map/ppermute | solution.py:95
  83.9 89.2 %copy-start.18 = (pred[1024]{0:T(1024)(128)(4,1)}, pred[1024]{0:T(1024)(128)(4,1)S(1)}, u32[]{:S(2)}) copy-start(pred[1024]{0:T(1024)(128)(4,1)S(1)} %get-tuple-element.328) | copy-start | bytes 3076
  83.9 89.2 %copy-start.20 = (pred[1024]{0:T(1024)(128)(4,1)}, pred[1024]{0:T(1024)(128)(4,1)S(1)}, u32[]{:S(2)}) copy-start(pred[1024]{0:T(1024)(128)(4,1)S(1)} %get-tuple-element.329) | copy-start | bytes 3076
  90.7 8.9 %collective-permute-start.4 = (bf16[1,256,256]{1,2,0:T(8,128)(2,1)S(1)}, bf16[1,256,256]{1,2,0:T(8,128)(2,1)S(1)}, u32[]{:S(2)}, u32[]{:S(2)}) collective-permute-start(bf16[1,256,256]{1,2,0:T(8,128)(2,1)S(1)} %get-tuple-element.318), channel_id=1, source_target_pairs={{0,1},{1,2},{2,3},{3,0},{4,5},{5,6},{6,7},{7,4},{8,9},{9,10},{10,1... | collective-permute-start | bytes 393224 | tf_op jit(solution)/shard_map/ppermute | solution.py:32
  92.1 7.4 %collective-permute-start.3 = (bf16[1,256,256]{1,2,0:T(8,128)(2,1)S(1)}, bf16[1,256,256]{1,2,0:T(8,128)(2,1)S(1)}, u32[]{:S(2)}, u32[]{:S(2)}) collective-permute-start(bf16[1,256,256]{1,2,0:T(8,128)(2,1)S(1)} %get-tuple-element.319), channel_id=1, source_target_pairs={{1,0},{2,1},{3,2},{0,3},{5,4},{6,5},{7,6},{4,7},{9,8},{10,9},{11,1... | collective-permute-start | bytes 393224 | tf_op jit(solution)/shard_map/ppermute | solution.py:33
  133.5 11.5 %collective-permute-start.6 = (bf16[1,256,256]{1,2,0:T(8,128)(2,1)S(1)}, bf16[1,256,256]{1,2,0:T(8,128)(2,1)S(1)}, u32[]{:S(2)}, u32[]{:S(2)}) collective-permute-start(bf16[1,256,256]{1,2,0:T(8,128)(2,1)S(1)} %get-tuple-element.252), channel_id=1, source_target_pairs={{0,1},{1,2},{2,3},{3,0},{4,5},{5,6},{6,7},{7,4},{8,9},{9,10},{10,1... | collective-permute-start | bytes 393224 | tf_op jit(solution)/shard_map/ppermute | solution.py:32
  133.9 10.9 %collective-permute-start.5 = (bf16[1,256,256]{1,2,0:T(8,128)(2,1)S(1)}, bf16[1,256,256]{1,2,0:T(8,128)(2,1)S(1)}, u32[]{:S(2)}, u32[]{:S(2)}) collective-permute-start(bf16[1,256,256]{1,2,0:T(8,128)(2,1)S(1)} %get-tuple-element.253), channel_id=1, source_target_pairs={{1,0},{2,1},{3,2},{0,3},{5,4},{6,5},{7,6},{4,7},{9,8},{10,9},{11,1... | collective-permute-start | bytes 393224 | tf_op jit(solution)/shard_map/ppermute | solution.py:33
  144.8 82.8 %reduce-scatter.9.cloned.1.call-start = ((), (), s32[]{:S(2)}) async-start(), calls=%async_computation.6 | async-start | bytes 1474560 | tf_op jit(solution)/shard_map/reduce_scatter | solution.py:157
  180.0 7.7 %collective-permute-start.8 = (bf16[1,256,256]{1,2,0:T(8,128)(2,1)}, bf16[1,256,256]{1,2,0:T(8,128)(2,1)S(1)}, u32[]{:S(2)}, u32[]{:S(2)}) collective-permute-start(bf16[1,256,256]{1,2,0:T(8,128)(2,1)} %get-tuple-element.186), channel_id=1, source_target_pairs={{0,1},{1,2},{2,3},{3,0},{4,5},{5,6},{6,7},{7,4},{8,9},{9,10},{10,1... | collective-permute-start | bytes 393224 | tf_op jit(solution)/shard_map/ppermute | solution.py:32
  180.0 7.6 %collective-permute-start.7 = (bf16[1,256,256]{1,2,0:T(8,128)(2,1)}, bf16[1,256,256]{1,2,0:T(8,128)(2,1)S(1)}, u32[]{:S(2)}, u32[]{:S(2)}) collective-permute-start(bf16[1,256,256]{1,2,0:T(8,128)(2,1)} %get-tuple-element.187), channel_id=1, source_target_pairs={{1,0},{2,1},{3,2},{0,3},{5,4},{6,5},{7,6},{4,7},{9,8},{10,9},{11,1... | collective-permute-start | bytes 393224 | tf_op jit(solution)/shard_map/ppermute | solution.py:33
  186.3 1.0 copy-start.11
  187.3 60.1 %reduce-scatter.7.cloned.1.call-start = ((), (), s32[]{:S(2)}) async-start(), calls=%async_computation.5 | async-start | bytes 1474560 | tf_op jit(solution)/shard_map/reduce_scatter | solution.py:157
  190.2 0.7 copy-start.22
  190.2 0.7 copy-start.31
  190.9 3.0 copy-start.39
  193.9 2.6 copy-start.19
  193.9 2.6 copy-start.21
  195.4 4.1 %copy-start.9 = (bf16[256,1024]{0,1:T(8,128)(2,1)}, bf16[256,1024]{0,1:T(8,128)(2,1)S(1)}, u32[]{:S(2)}) copy-start(bf16[256,1024]{0,1:T(8,128)(2,1)S(1)} %get-tuple-element.117) | copy-start | bytes 1572868
  195.4 18.3 %copy-start.7 = (bf16[256,1024]{0,1:T(8,128)(2,1)}, bf16[256,1024]{0,1:T(8,128)(2,1)S(1)}, u32[]{:S(2)}) copy-start(bf16[256,1024]{0,1:T(8,128)(2,1)S(1)} %get-tuple-element.116) | copy-start | bytes 1572868
  196.5 4.0 %copy-start.29 = (bf16[1,256,1,1,1,1,4]{1,6,5,4,3,2,0:T(4,128)(2,1)S(1)}, bf16[1,256,1,1,1,1,4]{1,6,5,4,3,2,0:T(4,128)(2,1)}, u32[]{:S(2)}) copy-start(bf16[1,256,1,1,1,1,4]{1,6,5,4,3,2,0:T(4,128)(2,1)} %get-tuple-element.164) | copy-start | bytes 6148
  196.5 4.0 %copy-start.30 = (bf16[1,256,1,1,1,1,3]{1,6,5,4,3,2,0:T(4,128)(2,1)S(1)}, bf16[1,256,1,1,1,1,3]{1,6,5,4,3,2,0:T(4,128)(2,1)}, u32[]{:S(2)}) copy-start(bf16[1,256,1,1,1,1,3]{1,6,5,4,3,2,0:T(4,128)(2,1)} %get-tuple-element.152) | copy-start | bytes 4612
  196.5 4.0 %copy-start.35 = (bf16[1,256,1,1,1,1,2]{1,6,5,4,3,2,0:T(2,128)(2,1)S(1)}, bf16[1,256,1,1,1,1,2]{1,6,5,4,3,2,0:T(2,128)(2,1)}, u32[]{:S(2)}) copy-start(bf16[1,256,1,1,1,1,2]{1,6,5,4,3,2,0:T(2,128)(2,1)} %get-tuple-element.140) | copy-start | bytes 3076
  203.6 2.1 copy-start.27
  203.6 2.1 copy-start.28
  203.6 2.1 copy-start.34
  208.7 4.0 %copy-start.3 = (bf16[256,1024]{0,1:T(8,128)(2,1)}, bf16[256,1024]{0,1:T(8,128)(2,1)S(1)}, u32[]{:S(2)}) copy-start(bf16[256,1024]{0,1:T(8,128)(2,1)S(1)} %fusion.312) | copy-start | bytes 1572868
  212.7 2.0 copy-start.5
  212.7 2.0 copy-start.25
  212.7 2.0 copy-start.26
  212.7 2.0 copy-start.33
  217.7 2.3 copy-start.10
  218.8 88.8 %all-reduce.3.cloned.1.call-start = ((), (), s32[]{:S(2)}) async-start(), calls=%async_computation.8 | async-start | bytes 1769472 | tf_op jit(solution)/shard_map/psum | solution.py:160
  222.5 2.6 copy-start.4
  223.7 2.5 copy-start.6
  226.2 21.2 %copy-start.8 = (bf16[256,1024]{0,1:T(8,128)(2,1)S(1)}, bf16[256,1024]{0,1:T(8,128)(2,1)}, u32[]{:S(2)}) copy-start(bf16[256,1024]{0,1:T(8,128)(2,1)} %copy-done.7) | copy-start | bytes 1572868
  248.6 61.4 %copy-start.1 = (f32[2,12,64,64]{3,2,1,0:T(8,128)S(1)}, f32[2,12,64,64]{3,2,1,0:T(8,128)}, u32[]{:S(2)}) copy-start(f32[2,12,64,64]{3,2,1,0:T(8,128)} %param.12) | copy-start | bytes 1179652
  (6 other events, 4.0 us)
Sparse Core Ops, SparseCore 0:
  11.2 55.3 reduce-scatter.4
  144.9 27.6 reduce-scatter.10
  187.4 27.6 reduce-scatter.8
  218.9 28.4 reduce-scatter.6
  250.0 57.5 all-reduce.2
